TPU v7x, 32 devices: a whole 2x2x4 slice. The times are simulated.
32 devices in a mesh: sub: 8 (over y, x, core), grp: 4 (over z).
Axes of the slice: x: 2, y: 2, z: 4, core: 2. Of those that a mesh axis runs over, the one named last changes fastest.
Arguments:
- res_inner: bfloat16 [2048, 16, 144], P(('sub', 'grp')), may hold values from -6 to 6
- res_face: bfloat16 [1024, 16, 144], P(('sub', 'grp')), may hold values from -6 to 6
- inner_inv: bfloat16 [2048, 144, 144], P(('sub', 'grp')), may hold values from -0.5 to 0.5
- face_coupling: bfloat16 [1024, 144, 144], P(('sub', 'grp')), may hold values from -0.5 to 0.5
- face_elem: int32 [32, 32], P(('sub', 'grp')), may hold values from 0 to 63
- face_inv: bfloat16 [1024, 144, 144], P(('sub', 'grp')), may hold values from -0.5 to 0.5
- coarse_basis: bfloat16 [1024, 64, 144], P(('sub', 'grp')), may hold values from -0.0625 to 0.0625
- coarse_map: int32 [32, 64], P(('sub', 'grp')), may hold values from 0 to 511
- coarse_inv: float32 [512, 512], P('grp'), as said below
- recv_index: int32 [32, 32], P(('sub', 'grp')), may hold values from 0 to 8, as said below
- sharers: int32 [32, 32], P(('sub', 'grp')), may hold values from 0 to 32, as said below
Outputs:
- inner_out: bfloat16 [2048, 16, 144], P(('sub', 'grp'))
- face_out: bfloat16 [1024, 16, 144], P(('sub', 'grp'))
Inputs may be any that keep to these rules, and one draw needn't show every extreme that they name: `recv_index`: row o gives, for each subdomain s at position s, the index among the 8 blocks owned by subdomain o that slot o of subdomain s refers to, or 8 where that slot is unused. `sharers`: for a used slot, the number of used slots of all subdomains that refer to the same owned block, up to all 32 of them, which some block reaches; 0 exactly for unused slots. coarse_inv is symmetric.
All inputs are finite; a program needn't handle non-finite values.
Results may differ from a plain program's by a relative error of at most 0.006.
Values may be sent and summed in bfloat16 or wider, within the bound.
No kernel may reach another device: no remote copies, remote signals or barrier semaphores. Data moves between devices by JAX's collectives and lax.ppermute only.
A program may use at most 128 MiB of HBM per device.

v0:
```python
import jax
import jax.numpy as jnp
from jax import lax
from jax.sharding import PartitionSpec as P


def send_out(partials):
    return lax.all_to_all(partials, ("sub", "grp"), split_axis=0, concat_axis=0, tiled=True)


def send_back(spread):
    return lax.all_to_all(spread, ("sub", "grp"), split_axis=0, concat_axis=0, tiled=True)


def body(
    res_inner,
    res_face,
    inner_inv,
    face_coupling,
    face_elem,
    face_inv,
    coarse_basis,
    coarse_map,
    coarse_inv,
    recv_index,
    sharers,
):
    num_faces = res_face.shape[0]
    num_owned = num_faces // 4
    elements = res_inner.shape[0]
    num_coarse = coarse_inv.shape[1]
    counts = sharers[0]
    weights = jnp.where(counts > 0, 1.0 / jnp.maximum(counts, 1).astype(jnp.float32), 0.0)
    owner_onehot = (
        recv_index[0][None, :] == jnp.arange(num_owned, dtype=jnp.int32)[:, None]
    ).astype(jnp.bfloat16)

    def assemble(partials):
        received = send_out(partials)
        flattened = received.reshape(num_faces, -1)
        owner_sum = jnp.dot(owner_onehot, flattened, preferred_element_type=jnp.float32).astype(
            jnp.bfloat16
        )
        spread = jnp.einsum(
            "of,ok->fk", owner_onehot, owner_sum, preferred_element_type=jnp.float32
        ).astype(jnp.bfloat16)
        return send_back(spread.reshape(partials.shape))

    inner_w = jnp.einsum(
        "erb,ecb->erc", res_inner, inner_inv, preferred_element_type=jnp.float32
    ).astype(jnp.bfloat16)
    nearby = inner_w[face_elem[0]]
    condensed = res_face.astype(jnp.float32) - jnp.einsum(
        "lrb,lcb->lrc", nearby, face_coupling, preferred_element_type=jnp.float32
    )
    sent = (weights[:, None, None] * condensed).astype(jnp.bfloat16)
    gathered = assemble(sent)
    restricted = (weights[:, None, None] * gathered.astype(jnp.float32)).astype(jnp.bfloat16)
    local_coarse = jnp.einsum(
        "ljb,lrb->jr", coarse_basis, restricted, preferred_element_type=jnp.float32
    )
    coarse_onehot = (
        coarse_map[0][None, :] == jnp.arange(num_coarse, dtype=jnp.int32)[:, None]
    ).astype(jnp.float32)
    partial_rhs = jnp.dot(coarse_onehot, local_coarse, precision=lax.Precision.HIGHEST)
    coarse_rhs = lax.psum(partial_rhs, ("sub", "grp"))
    row_part = jnp.dot(coarse_inv, coarse_rhs, precision=lax.Precision.HIGHEST)
    coarse_sol = lax.all_gather(row_part, "grp", axis=0, tiled=True)
    picked = jnp.einsum(
        "kj,kr->jr", coarse_onehot, coarse_sol, precision=lax.Precision.HIGHEST
    ).astype(jnp.bfloat16)
    coarse_part = jnp.einsum(
        "ljb,jr->lrb", coarse_basis, picked, preferred_element_type=jnp.float32
    )
    local_part = jnp.einsum(
        "lrb,lcb->lrc", restricted, face_inv, preferred_element_type=jnp.float32
    )
    weighted = (weights[:, None, None] * (coarse_part + local_part)).astype(jnp.bfloat16)
    face_out = assemble(weighted)
    contrib = jnp.einsum(
        "lrc,lcb->lrb", face_out, face_coupling, preferred_element_type=jnp.float32
    )
    elem_onehot = (face_elem[0][None, :] == jnp.arange(elements, dtype=jnp.int32)[:, None]).astype(
        jnp.float32
    )
    scattered = jnp.dot(
        elem_onehot, contrib.reshape(num_faces, -1), precision=lax.Precision.HIGHEST
    ).reshape(res_inner.shape)
    inner_rhs = (res_inner.astype(jnp.float32) - scattered).astype(jnp.bfloat16)
    inner_out = jnp.einsum(
        "erb,ecb->erc", inner_rhs, inner_inv, preferred_element_type=jnp.float32
    ).astype(jnp.bfloat16)
    return (inner_out, face_out)


def solution(mesh):
    return jax.shard_map(
        body,
        mesh=mesh,
        in_specs=(
            P(("sub", "grp"), None, None),
            P(("sub", "grp"), None, None),
            P(("sub", "grp"), None, None),
            P(("sub", "grp"), None, None),
            P(("sub", "grp"), None),
            P(("sub", "grp"), None, None),
            P(("sub", "grp"), None, None),
            P(("sub", "grp"), None),
            P("grp", None),
            P(("sub", "grp"), None),
            P(("sub", "grp"), None),
        ),
        out_specs=(P(("sub", "grp"), None, None), P(("sub", "grp"), None, None)),
        check_vma=False,
    )
```

profile of v0, /device:TPU:0, one launch (start us, length us, event | category | flops | bytes accessed | tf_op | source)
XLA Modules:
  0.0 140.8 jit_solution(13594599169915256372)
XLA Ops:
  0.6 0.8 fusion.20
  1.5 0.7 fusion.19
  2.1 3.8 %convolution_convert_fusion.5 = bf16[64,16,144]{2,1,0:T(8,128)(2,1)S(1)} fusion(bf16[64,16,144]{2,1,0:T(8,128)(2,1)} %param.11, bf16[64,144,144]{2,1,0:T(8,128)(2,1)} %param.13), kind=kOutput, calls=%fused_computation.6 | convolution fusion | flops 42614784 | bytes 3244032 | tf_op jit(solution)/shard_map/erb,ecb->erc/dot_general | solution.py:49
  6.0 1.3 gather_fusion
  7.3 1.8 %fusion.2 = bf16[32,16,144]{2,1,0:T(8,128)(2,1)S(1)} fusion(bf16[32,16,144]{2,1,0:T(8,128)(2,1)} %gather_fusion, bf16[32,144,144]{2,1,0:T(8,128)(2,1)S(1)} %copy-done, bf16[32,16,144]{2,1,0:T(8,128)(2,1)} %param.12, f32[32]{0:T(128)S(1)} %fusion.20), kind=kOutput, calls=%fused_computation.12 | convolution fusion | flops 21528576 | bytes 1769600 | tf_op jit(solution)/shard_map/lrb,lcb->lrc/dot_general | solution.py:53
  9.1 17.5 %all_to_all.20 = bf16[32,16,144]{2,1,0:T(8,128)(2,1)} all-to-all(bf16[32,16,144]{2,1,0:T(8,128)(2,1)S(1)} %fusion.2), channel_id=1, replica_groups=mesh['sub'=8,'grp'=4] {'sub','grp'}, dimensions={0} | all-to-all | bytes 294912 | tf_op jit(solution)/shard_map/all_to_all | solution.py:8
  26.6 1.3 reshape.70
  27.9 1.7 %convolution_convert_fusion.1 = bf16[32,2304]{1,0:T(8,128)(2,1)} fusion(bf16[32,2304]{1,0:T(8,128)(2,1)S(1)} %reshape.70, s32[32]{0:T(128)} %bitcast.41), kind=kOutput, calls=%fused_computation.2 | convolution fusion | flops 2451968 | bytes 295040 | tf_op jit(solution)/shard_map/of,ok->fk/dot_general | solution.py:44
  29.5 2.0 %reshape.71 = bf16[32,16,144]{2,1,0:T(8,128)(2,1)} reshape(bf16[32,2304]{1,0:T(8,128)(2,1)} %convolution_convert_fusion.1) | data formatting | bytes 294912 | tf_op jit(solution)/shard_map/reshape | solution.py:47
  31.6 12.9 %all_to_all.21 = bf16[32,16,144]{2,1,0:T(8,128)(2,1)S(1)} all-to-all(bf16[32,16,144]{2,1,0:T(8,128)(2,1)} %reshape.71), channel_id=1, replica_groups=mesh['sub'=8,'grp'=4] {'sub','grp'}, dimensions={0} | all-to-all | bytes 294912 | tf_op jit(solution)/shard_map/all_to_all | solution.py:12
  44.5 0.7 copy-done.2
  45.2 1.1 convolution_bitcast_fusion.1
  46.3 1.6 %fusion.9 = f32[512,16]{1,0:T(8,128)} fusion(f32[16,64]{1,0:T(8,128)S(1)} %convolution_bitcast_fusion.1, s32[64]{0:T(128)} %bitcast.43), kind=kOutput, calls=%fused_computation.24 | convolution fusion | flops 6324224 | bytes 37120 | tf_op jit(solution)/shard_map/dot_general | solution.py:65
  47.9 41.1 %psum.7 = f32[512,16]{1,0:T(8,128)} all-reduce(f32[512,16]{1,0:T(8,128)} %fusion.9), channel_id=1, replica_groups=mesh['sub'=8,'grp'=4] {'sub','grp'}, use_global_device_ids=true, to_apply=%region_0.1 | all-reduce | flops 8192 | bytes 65536 | tf_op jit(solution)/shard_map/psum | solution.py:66
  89.0 1.6 %convolution_bitcast_fusion.2 = f32[128,16]{0,1:T(8,128)S(1)} fusion(f32[512,16]{1,0:T(8,128)} %psum.7, f32[128,512]{1,0:T(8,128)} %param.19), kind=kOutput, calls=%fused_computation.15 | convolution fusion | flops 12582912 | bytes 303104 | tf_op jit(solution)/shard_map/dot_general | solution.py:67
  90.7 13.1 %all_gather.3 = f32[512,16]{0,1:T(8,128)S(1)} all-gather(f32[128,16]{0,1:T(8,128)S(1)} %convolution_bitcast_fusion.2), channel_id=1, replica_groups=mesh['sub'=8,'grp'=4] {'grp'}, dimensions={0}, use_global_device_ids=true | all-gather | bytes 40960 | tf_op jit(solution)/shard_map/all_gather | solution.py:68
  104.3 2.4 %fusion.3 = bf16[32,16,144]{2,1,0:T(8,128)(2,1)S(1)} fusion(f32[32,16,144]{2,1,0:T(8,128)S(1)} %convolution_bitcast_fusion, bf16[32,144,144]{2,1,0:T(8,128)(2,1)} %param.16, f32[32]{0:T(128)S(1)} %copy-done.6, bf16[32,16,144]{2,1,0:T(8,128)(2,1)S(1)} %copy-done.3), kind=kOutput, calls=%fused_computation.13 | convolution fusion | flops 21676032 | bytes 1917056 | tf_op jit(solution)/shard_map/lrb,lcb->lrc/dot_general | solution.py:75
  106.7 13.0 %all_to_all.22 = bf16[32,16,144]{2,1,0:T(8,128)(2,1)S(1)} all-to-all(bf16[32,16,144]{2,1,0:T(8,128)(2,1)S(1)} %fusion.3), channel_id=1, replica_groups=mesh['sub'=8,'grp'=4] {'sub','grp'}, dimensions={0} | all-to-all | bytes 294912 | tf_op jit(solution)/shard_map/all_to_all | solution.py:8
  120.3 0.4 reshape.73
  120.7 12.7 %all_to_all.23 = bf16[32,16,144]{2,1,0:T(8,128)(2,1)S(1)} all-to-all(bf16[32,16,144]{2,1,0:T(8,128)(2,1)S(1)} %reshape.73), channel_id=1, replica_groups=mesh['sub'=8,'grp'=4] {'sub','grp'}, dimensions={0} | all-to-all | bytes 294912 | tf_op jit(solution)/shard_map/all_to_all | solution.py:12
  133.4 0.4 fusion.21
  134.5 0.9 fusion.7
  135.4 4.7 %convolution_convert_fusion.4 = bf16[64,16,144]{2,1,0:T(8,128)(2,1)} fusion(bf16[64,144,144]{2,1,0:T(8,128)(2,1)} %param.13, f32[64,16,144]{2,0,1:T(8,128)S(1)} %fusion.7, bf16[64,16,144]{2,1,0:T(8,128)(2,1)} %param.11), kind=kOutput, calls=%fused_computation.5 | convolution fusion | flops 43057152 | bytes 3833856 | tf_op jit(solution)/shard_map/erb,ecb->erc/dot_general | solution.py:90
  140.1 0.7 copy.22
  (24 shorter events, 1.7 us)
Async XLA Ops:
  0.6 6.6 %copy-start = (bf16[32,144,144]{2,1,0:T(8,128)(2,1)S(1)}, bf16[32,144,144]{2,1,0:T(8,128)(2,1)}, u32[]{:S(2)}) copy-start(bf16[32,144,144]{2,1,0:T(8,128)(2,1)} %param.14) | copy-start | bytes 3981316
  1.5 5.8 %copy-start.5 = (f32[32]{0:T(128)}, f32[32]{0:T(128)S(1)}, u32[]{:S(2)}) copy-start(f32[32]{0:T(128)S(1)} %fusion.20) | copy-start | bytes 388
  7.3 38.0 %copy-start.1 = (bf16[32,64,144]{2,1,0:T(8,128)(2,1)S(1)}, bf16[32,64,144]{2,1,0:T(8,128)(2,1)}, u32[]{:S(2)}) copy-start(bf16[32,64,144]{2,1,0:T(8,128)(2,1)} %param.17) | copy-start | bytes 1769476
  29.5 74.3 %copy-start.7 = (s32[1,64]{1,0:T(1,128)S(1)}, s32[1,64]{1,0:T(1,128)}, u32[]{:S(2)}) copy-start(s32[1,64]{1,0:T(1,128)} %param.18) | copy-start | bytes 772
  31.6 72.7 %copy-start.6 = (f32[32]{0:T(128)S(1)}, f32[32]{0:T(128)}, u32[]{:S(2)}) copy-start(f32[32]{0:T(128)} %copy-done.5) | copy-start | bytes 388
  44.5 0.7 copy-start.2
  89.0 15.2 %copy-start.3 = (bf16[32,16,144]{2,1,0:T(8,128)(2,1)S(1)}, bf16[32,16,144]{2,1,0:T(8,128)(2,1)}, u32[]{:S(2)}) copy-start(bf16[32,16,144]{2,1,0:T(8,128)(2,1)} %copy-done.2) | copy-start | bytes 442372
  104.3 15.7 %copy-start.4 = (s32[1,32]{1,0:T(1,128)S(1)}, s32[1,32]{1,0:T(1,128)}, u32[]{:S(2)}) copy-start(s32[1,32]{1,0:T(1,128)} %param.20) | copy-start | bytes 388
  133.4 1.1 copy-start.8
where the time goes:
time: 141 us
  blocking collectives  110 us (78%)
  matrix products  20.8 us (15%)
  local copies, waits for them, and re-layouts  7.45 us (5%)
  other arithmetic  1.48 us (1%)
    psum x1, blocking collectives, body(): coarse_rhs = lax.psum(partial_rhs, ('sub', 'grp'))  41.1 us
    all_to_all x2, blocking collectives, send_out(): lax.all_to_all(partials, ('sub', 'grp'), split_axis=0, concat_axis=0, til...  30.4 us
    all_to_all x2, blocking collectives, send_back(): lax.all_to_all(spread, ('sub', 'grp'), split_axis=0, concat_axis=0, tiled...  25.6 us
    all_gather x1, blocking collectives, body(): coarse_sol = lax.all_gather(row_part, 'grp', axis=0, tiled=True)  13.1 us
    dot_general x1, matrix products, body(): jnp.einsum('erb,ecb->erc', inner_rhs, inner_inv, preferred_element_type=j...  4.68 us
    dot_general x1, matrix products, body(): jnp.einsum('erb,ecb->erc', res_inner, inner_inv, preferred_element_type=j...  3.82 us

commit v1 on v0

--- a/solution.py
+++ b/solution.py
@@ -2,6 +2,18 @@
 import jax.numpy as jnp
 from jax import lax
 from jax.sharding import PartitionSpec as P
+
+
+def doubled_up(x, axis, dim):
+    ways, here = (lax.axis_size(axis), lax.axis_index(axis))
+    grown, reach = (x, 1)
+    while reach < ways:
+        theirs = lax.ppermute(grown, axis, [(d, d ^ reach) for d in range(ways)])
+        mine_first = jnp.concatenate([grown, theirs], axis=dim)
+        theirs_first = jnp.concatenate([theirs, grown], axis=dim)
+        grown = jnp.where(here & reach == 0, mine_first, theirs_first)
+        reach = 2 * reach
+    return grown
 
 
 def send_out(partials):
@@ -65,7 +77,7 @@
     partial_rhs = jnp.dot(coarse_onehot, local_coarse, precision=lax.Precision.HIGHEST)
     coarse_rhs = lax.psum(partial_rhs, ("sub", "grp"))
     row_part = jnp.dot(coarse_inv, coarse_rhs, precision=lax.Precision.HIGHEST)
-    coarse_sol = lax.all_gather(row_part, "grp", axis=0, tiled=True)
+    coarse_sol = doubled_up(row_part, "grp", 0)
     picked = jnp.einsum(
         "kj,kr->jr", coarse_onehot, coarse_sol, precision=lax.Precision.HIGHEST
     ).astype(jnp.bfloat16)

time: 141 us -> 137 us (0.972)
  blocking collectives: 110 us -> 97.3 us
  waiting for transfers between devices: 0 us -> 5.34 us
  starting transfers between devices: 0 us -> 2.97 us
    all_gather x1 -> x0, blocking collectives: 13.1 us -> none  [body(): coarse_sol = lax.all_gather(row_part, 'grp', axis=0, tiled=True)]
    ppermute x0 -> x2, waiting for transfers between devices: none -> 5.34 us  [doubled_up(): theirs = lax.ppermute(grown, axis, [(d, d ^ reach) for d in range(ways)])]
    ppermute x0 -> x2, starting transfers between devices: none -> 2.97 us  [doubled_up(): theirs = lax.ppermute(grown, axis, [(d, d ^ reach) for d in range(ways)])]
  transfers between devices with their start and end apart: 0 -> 2, of which waited for: 0 -> 2; matrix products, arithmetic and copies ran while one was open for 0% -> 0% of each run, Pallas kernels for 0% -> 0%
where the time goes in v1:
time: 137 us; the launch traced here: 136 us
  blocking collectives  97.3 us (71%)
  matrix products  20.9 us (15%)
  local copies, waits for them, and re-layouts  7.45 us (5%)
  waiting for transfers between devices  5.34 us (4%)
  starting transfers between devices  2.97 us (2%)
  other arithmetic  1.49 us (1%)
    psum x1, blocking collectives, body(): coarse_rhs = lax.psum(partial_rhs, ('sub', 'grp'))  41.1 us
    all_to_all x2, blocking collectives, send_out(): lax.all_to_all(partials, ('sub', 'grp'), split_axis=0, concat_axis=0, til...  30.5 us
    all_to_all x2, blocking collectives, send_back(): lax.all_to_all(spread, ('sub', 'grp'), split_axis=0, concat_axis=0, tiled...  25.6 us
    ppermute x2, waiting for transfers between devices, doubled_up(): theirs = lax.ppermute(grown, axis, [(d, d ^ reach) for d in range(ways)])  5.34 us
    dot_general x1, matrix products, body(): jnp.einsum('erb,ecb->erc', inner_rhs, inner_inv, preferred_element_type=j...  4.68 us
    dot_general x1, matrix products, body(): jnp.einsum('erb,ecb->erc', res_inner, inner_inv, preferred_element_type=j...  3.82 us
    ppermute x2, starting transfers between devices, doubled_up(): theirs = lax.ppermute(grown, axis, [(d, d ^ reach) for d in range(ways)])  2.97 us
  transfers between devices with their start and end apart: 2, of which 2 were waited for; matrix products, arithmetic and copies ran while one was open for 0% of the time, Pallas kernels for 0%

profile of v1, /device:TPU:0, one launch (start us, length us, event | category | flops | bytes accessed | tf_op | source)
XLA Modules:
  0.0 136.1 jit_solution(17147260302834455358)
XLA Ops:
  0.6 0.8 fusion.26
  2.1 3.8 %convolution_convert_fusion.5 = bf16[64,16,144]{2,1,0:T(8,128)(2,1)S(1)} fusion(bf16[64,16,144]{2,1,0:T(8,128)(2,1)} %param.11, bf16[64,144,144]{2,1,0:T(8,128)(2,1)} %param.13), kind=kOutput, calls=%fused_computation.6 | convolution fusion | flops 42614784 | bytes 3244032 | tf_op jit(solution)/shard_map/erb,ecb->erc/dot_general | solution.py:61
  6.0 1.3 gather_fusion
  7.3 1.8 %fusion.2 = bf16[32,16,144]{2,1,0:T(8,128)(2,1)S(1)} fusion(bf16[32,16,144]{2,1,0:T(8,128)(2,1)} %gather_fusion, bf16[32,144,144]{2,1,0:T(8,128)(2,1)S(1)} %copy-done, bf16[32,16,144]{2,1,0:T(8,128)(2,1)} %param.12, f32[32]{0:T(128)S(1)} %fusion.26), kind=kOutput, calls=%fused_computation.12 | convolution fusion | flops 21528576 | bytes 1769600 | tf_op jit(solution)/shard_map/lrb,lcb->lrc/dot_general | solution.py:65
  9.1 17.5 %all_to_all.20 = bf16[32,16,144]{2,1,0:T(8,128)(2,1)} all-to-all(bf16[32,16,144]{2,1,0:T(8,128)(2,1)S(1)} %fusion.2), channel_id=1, replica_groups=mesh['sub'=8,'grp'=4] {'sub','grp'}, dimensions={0} | all-to-all | bytes 294912 | tf_op jit(solution)/shard_map/all_to_all | solution.py:20
  26.6 1.3 reshape.70
  27.9 1.7 %convolution_convert_fusion.1 = bf16[32,2304]{1,0:T(8,128)(2,1)} fusion(bf16[32,2304]{1,0:T(8,128)(2,1)S(1)} %reshape.70, s32[32]{0:T(128)} %bitcast.40), kind=kOutput, calls=%fused_computation.2 | convolution fusion | flops 2451968 | bytes 295040 | tf_op jit(solution)/shard_map/of,ok->fk/dot_general | solution.py:56
  29.5 2.0 %reshape.71 = bf16[32,16,144]{2,1,0:T(8,128)(2,1)} reshape(bf16[32,2304]{1,0:T(8,128)(2,1)} %convolution_convert_fusion.1) | data formatting | bytes 294912 | tf_op jit(solution)/shard_map/reshape | solution.py:59
  31.6 12.9 %all_to_all.21 = bf16[32,16,144]{2,1,0:T(8,128)(2,1)S(1)} all-to-all(bf16[32,16,144]{2,1,0:T(8,128)(2,1)} %reshape.71), channel_id=1, replica_groups=mesh['sub'=8,'grp'=4] {'sub','grp'}, dimensions={0} | all-to-all | bytes 294912 | tf_op jit(solution)/shard_map/all_to_all | solution.py:24
  44.5 0.7 copy-done.2
  45.2 1.1 convolution_bitcast_fusion.1
  46.3 1.6 %fusion.9 = f32[512,16]{1,0:T(8,128)} fusion(f32[16,64]{1,0:T(8,128)S(1)} %convolution_bitcast_fusion.1, s32[64]{0:T(128)} %bitcast.42), kind=kOutput, calls=%fused_computation.24 | convolution fusion | flops 6324224 | bytes 37120 | tf_op jit(solution)/shard_map/dot_general | solution.py:77
  47.9 41.1 %psum.7 = f32[512,16]{1,0:T(8,128)} all-reduce(f32[512,16]{1,0:T(8,128)} %fusion.9), channel_id=1, replica_groups=mesh['sub'=8,'grp'=4] {'sub','grp'}, use_global_device_ids=true, to_apply=%region_0.1 | all-reduce | flops 8192 | bytes 65536 | tf_op jit(solution)/shard_map/psum | solution.py:78
  89.1 1.6 %convolution_bitcast_fusion.2 = f32[128,16]{0,1:T(8,128)S(1)} fusion(f32[512,16]{1,0:T(8,128)} %psum.7, f32[128,512]{1,0:T(8,128)} %param.19), kind=kOutput, calls=%fused_computation.15 | convolution fusion | flops 12582912 | bytes 303104 | tf_op jit(solution)/shard_map/dot_general | solution.py:79
  90.7 1.3 collective-permute-start
  92.0 2.4 %collective-permute-done = f32[128,16]{0,1:T(8,128)S(1)} collective-permute-done((f32[128,16]{0,1:T(8,128)S(1)}, f32[128,16]{0,1:T(8,128)S(1)}, u32[]{:S(2)}, u32[]{:S(2)}) %collective-permute-start) | collective-permute-done | bytes 8224 | tf_op jit(solution)/shard_map/ppermute | solution.py:11
  94.3 1.7 %collective-permute-start.1 = (f32[256,16]{0,1:T(8,128)S(1)}, f32[256,16]{0,1:T(8,128)S(1)}, u32[]{:S(2)}, u32[]{:S(2)}) collective-permute-start(f32[256,16]{0,1:T(8,128)S(1)} %maximum_select_fusion.2), channel_id=1, source_target_pairs={{0,2},{1,3},{2,0},{3,1},{4,6},{5,7},{6,4},{7,5},{8,10},{9,11},{10,... | collective-permute-start | bytes 49160 | tf_op jit(solution)/shard_map/ppermute | solution.py:11
  96.0 3.0 %collective-permute-done.1 = f32[256,16]{0,1:T(8,128)S(1)} collective-permute-done((f32[256,16]{0,1:T(8,128)S(1)}, f32[256,16]{0,1:T(8,128)S(1)}, u32[]{:S(2)}, u32[]{:S(2)}) %collective-permute-start.1) | collective-permute-done | bytes 16416 | tf_op jit(solution)/shard_map/ppermute | solution.py:11
  99.5 2.5 %fusion.3 = bf16[32,16,144]{2,1,0:T(8,128)(2,1)S(1)} fusion(f32[32,16,144]{2,1,0:T(8,128)S(1)} %convolution_bitcast_fusion, bf16[32,144,144]{2,1,0:T(8,128)(2,1)} %param.16, f32[32]{0:T(128)S(1)} %copy-done.5, bf16[32,16,144]{2,1,0:T(8,128)(2,1)} %copy-done.2), kind=kOutput, calls=%fused_computation.13 | convolution fusion | flops 21676032 | bytes 1917056 | tf_op jit(solution)/shard_map/lrb,lcb->lrc/dot_general | solution.py:87
  102.0 13.0 %all_to_all.22 = bf16[32,16,144]{2,1,0:T(8,128)(2,1)S(1)} all-to-all(bf16[32,16,144]{2,1,0:T(8,128)(2,1)S(1)} %fusion.3), channel_id=1, replica_groups=mesh['sub'=8,'grp'=4] {'sub','grp'}, dimensions={0} | all-to-all | bytes 294912 | tf_op jit(solution)/shard_map/all_to_all | solution.py:20
  116.1 12.7 %all_to_all.23 = bf16[32,16,144]{2,1,0:T(8,128)(2,1)S(1)} all-to-all(bf16[32,16,144]{2,1,0:T(8,128)(2,1)S(1)} %reshape.73), channel_id=1, replica_groups=mesh['sub'=8,'grp'=4] {'sub','grp'}, dimensions={0} | all-to-all | bytes 294912 | tf_op jit(solution)/shard_map/all_to_all | solution.py:24
  129.8 0.9 fusion.7
  130.8 4.7 %convolution_convert_fusion.4 = bf16[64,16,144]{2,1,0:T(8,128)(2,1)} fusion(bf16[64,144,144]{2,1,0:T(8,128)(2,1)} %param.13, f32[64,16,144]{2,0,1:T(8,128)S(1)} %fusion.7, bf16[64,16,144]{2,1,0:T(8,128)(2,1)} %param.11), kind=kOutput, calls=%fused_computation.5 | convolution fusion | flops 43057152 | bytes 3833856 | tf_op jit(solution)/shard_map/erb,ecb->erc/dot_general | solution.py:102
  135.4 0.7 copy.22
  (26 shorter events, 3.3 us)
Async XLA Ops:
  0.6 6.6 %copy-start = (bf16[32,144,144]{2,1,0:T(8,128)(2,1)S(1)}, bf16[32,144,144]{2,1,0:T(8,128)(2,1)}, u32[]{:S(2)}) copy-start(bf16[32,144,144]{2,1,0:T(8,128)(2,1)} %param.14) | copy-start | bytes 3981316
  1.5 5.8 %copy-start.4 = (f32[32]{0:T(128)}, f32[32]{0:T(128)S(1)}, u32[]{:S(2)}) copy-start(f32[32]{0:T(128)S(1)} %fusion.26) | copy-start | bytes 388
  7.3 38.0 %copy-start.1 = (bf16[32,64,144]{2,1,0:T(8,128)(2,1)S(1)}, bf16[32,64,144]{2,1,0:T(8,128)(2,1)}, u32[]{:S(2)}) copy-start(bf16[32,64,144]{2,1,0:T(8,128)(2,1)} %param.17) | copy-start | bytes 1769476
  29.5 69.4 %copy-start.6 = (s32[1,64]{1,0:T(1,128)S(1)}, s32[1,64]{1,0:T(1,128)}, u32[]{:S(2)}) copy-start(s32[1,64]{1,0:T(1,128)} %param.18) | copy-start | bytes 772
  31.6 67.9 %copy-start.5 = (f32[32]{0:T(128)S(1)}, f32[32]{0:T(128)}, u32[]{:S(2)}) copy-start(f32[32]{0:T(128)} %copy-done.4) | copy-start | bytes 388
  44.5 0.7 copy-start.2
  90.7 3.7 %collective-permute-start = (f32[128,16]{0,1:T(8,128)S(1)}, f32[128,16]{0,1:T(8,128)S(1)}, u32[]{:S(2)}, u32[]{:S(2)}) collective-permute-start(f32[128,16]{0,1:T(8,128)S(1)} %convolution_bitcast_fusion.2), channel_id=1, source_target_pairs={{0,1},{1,0},{2,3},{3,2},{4,5},{5,4},{6,7},{7,6},{8,9},{9,8},{10,11... | collective-permute-start | bytes 24584 | tf_op jit(solution)/shard_map/ppermute | solution.py:11
  94.3 4.6 %collective-permute-start.1 = (f32[256,16]{0,1:T(8,128)S(1)}, f32[256,16]{0,1:T(8,128)S(1)}, u32[]{:S(2)}, u32[]{:S(2)}) collective-permute-start(f32[256,16]{0,1:T(8,128)S(1)} %maximum_select_fusion.2), channel_id=1, source_target_pairs={{0,2},{1,3},{2,0},{3,1},{4,6},{5,7},{6,4},{7,5},{8,10},{9,11},{10,... | collective-permute-start | bytes 49160 | tf_op jit(solution)/shard_map/ppermute | solution.py:11
  99.4 15.9 %copy-start.3 = (s32[1,32]{1,0:T(1,128)S(1)}, s32[1,32]{1,0:T(1,128)}, u32[]{:S(2)}) copy-start(s32[1,32]{1,0:T(1,128)} %param.20) | copy-start | bytes 388
  128.8 1.1 copy-start.7
